TPU v7x, 256 devices: a whole 4x4x8 slice. The times are simulated.
256 devices in a mesh: row: 32 (over z_lo, x, core), col: 8 (over z_hi, y).
Axes of the slice: x: 4, y: 4, z: 8 (z_hi: 2, z_lo: 4; z = z_hi * 4 + z_lo), core: 2. Of those that a mesh axis runs over, the one named last changes fastest.
Arguments:
- pair: bfloat16 [512, 512, 128], P('row', 'col'), may hold values from -6 to 6
- cotangent: bfloat16 [64, 512, 512], P(None, 'row', 'col'), may hold values from -0.59765625 to 0.59765625
- w_left: bfloat16 [128, 64], replicated, may hold values from -0.5 to 0.5
- w_left_gate: bfloat16 [128, 64], replicated, may hold values from -0.5 to 0.5
- w_right: bfloat16 [128, 64], replicated, may hold values from -0.5 to 0.5
- w_right_gate: bfloat16 [128, 64], replicated, may hold values from -0.5 to 0.5
Outputs:
- pair_gradient: bfloat16 [512, 512, 128], P('row', 'col')
- grad_left: float32 [128, 64], replicated
- grad_left_gate: float32 [128, 64], replicated
- grad_right: float32 [128, 64], replicated
- grad_right_gate: float32 [128, 64], replicated
All inputs are finite; a program needn't handle non-finite values.
Results may differ from a plain program's by a relative error of at most 0.0082.
Values may be sent and summed in bfloat16 or wider, within the bound.
A program may use at most 64 MiB of HBM per device.

v0:
```python
import jax
import jax.numpy as jnp
from jax import lax
from jax.sharding import PartitionSpec as P


def shards(pair, cotangent, w_left, w_left_gate, w_right, w_right_gate):
    pair_f = pair.astype(jnp.float32)
    average = jnp.mean(pair_f, axis=-1, keepdims=True)
    centered_input = pair_f - average
    variance = jnp.mean(centered_input * centered_input, axis=-1, keepdims=True)
    inverse_scale = 1.0 / jnp.sqrt(variance + 1e-05)
    standardized_input = centered_input * inverse_scale
    normalized_input = standardized_input.astype(jnp.bfloat16)
    stacked = jnp.concatenate([w_left, w_left_gate, w_right, w_right_gate], axis=1)
    projected = jnp.einsum(
        "rcd,dh->hrc", normalized_input, stacked, preferred_element_type=jnp.float32
    )
    q_left, p_left, q_right, p_right = jnp.split(projected, 4, axis=0)
    s_left = jax.nn.sigmoid(p_left)
    s_right = jax.nn.sigmoid(p_right)
    left = (s_left * q_left).astype(jnp.bfloat16)
    right = (s_right * q_right).astype(jnp.bfloat16)
    g_chan, left_chan, right_chan = (
        lax.all_to_all(cotangent, "col", split_axis=0, concat_axis=2, tiled=True),
        lax.all_to_all(left, "col", split_axis=0, concat_axis=2, tiled=True),
        lax.all_to_all(right, "col", split_axis=0, concat_axis=2, tiled=True),
    )
    residues = g_chan.shape[2]
    col_block = g_chan
    d_left = jnp.einsum(
        "hij,hjk->hik",
        col_block,
        lax.all_gather(right_chan, "row", axis=1, tiled=True),
        preferred_element_type=jnp.float32,
    )
    col_block = g_chan
    summed = lax.psum_scatter(
        jnp.einsum("hij,hik->jhk", col_block, left_chan, preferred_element_type=jnp.float32),
        "row",
        scatter_dimension=0,
        tiled=True,
    )
    d_right = jnp.transpose(summed, (1, 0, 2))
    d_left_tile, d_right_tile = (
        lax.all_to_all(d_left.astype(jnp.bfloat16), "col", split_axis=2, concat_axis=0, tiled=True),
        lax.all_to_all(
            d_right.astype(jnp.bfloat16), "col", split_axis=2, concat_axis=0, tiled=True
        ),
    )
    grad_l = d_left_tile.astype(jnp.float32)
    grad_r = d_right_tile.astype(jnp.float32)
    e_left = grad_l * s_left
    f_left = grad_l * q_left * s_left * (1.0 - s_left)
    e_right = grad_r * s_right
    f_right = grad_r * q_right * s_right * (1.0 - s_right)
    grads = jnp.concatenate([e_left, f_left, e_right, f_right], axis=0).astype(jnp.bfloat16)
    local_weights = jnp.einsum(
        "rcd,hrc->dh", normalized_input, grads, preferred_element_type=jnp.float32
    )
    total_weights = lax.psum(local_weights, ("row", "col")) / residues
    normalized_gradient = jnp.einsum(
        "hrc,dh->rcd", grads, stacked, preferred_element_type=jnp.float32
    )
    gradient_mean = jnp.mean(normalized_gradient, axis=-1, keepdims=True)
    gradient_input_mean = jnp.mean(normalized_gradient * standardized_input, axis=-1, keepdims=True)
    pair_gradient = (
        (normalized_gradient - gradient_mean - standardized_input * gradient_input_mean)
        * inverse_scale
    ).astype(jnp.bfloat16)
    pieces_w = jnp.split(total_weights, 4, axis=1)
    return (pair_gradient, pieces_w[0], pieces_w[1], pieces_w[2], pieces_w[3])


def solution(mesh):
    in_specs = (P("row", "col", None), P(None, "row", "col"), P(), P(), P(), P())
    out_specs = (P("row", "col", None), P(), P(), P(), P())
    return jax.shard_map(shards, mesh=mesh, in_specs=in_specs, out_specs=out_specs, check_vma=False)
```

profile of v0, /device:TPU:2, one launch (start us, length us, event | category | flops | bytes accessed | tf_op | source)
XLA Modules:
  0.0 579.7 jit_solution(9537658770375944991)
XLA Ops:
  7.2 1.2 convert_reduce_fusion
  8.4 1.3 fusion.10
  9.8 0.8 copy.87
  10.6 0.8 copy.88
  11.4 0.8 copy.89
  12.3 0.8 copy.90
  13.1 1.4 fusion.18
  14.6 0.2 multiply_convert_fusion.5
  14.8 0.3 copy.91
  15.1 0.2 reshape.47
  15.3 21.4 %all_to_all.72 = bf16[8,2,4096]{2,1,0:T(2,128)(2,1)S(1)} all-to-all(bf16[8,2,4096]{2,1,0:T(2,128)(2,1)S(1)} %reshape.47), channel_id=1, replica_groups=mesh['row'=32,'col'=8] {'col'}, dimensions={0} | all-to-all | bytes 262144 | tf_op jit(solution)/shard_map/all_to_all | solution.py:27
  37.1 0.9 all_to_all.56
  38.0 0.2 reshape.45
  38.3 13.0 %all_to_all.73 = bf16[8,2,4096]{2,1,0:T(2,128)(2,1)S(1)} all-to-all(bf16[8,2,4096]{2,1,0:T(2,128)(2,1)S(1)} %reshape.45), channel_id=1, replica_groups=mesh['row'=32,'col'=8] {'col'}, dimensions={0} | all-to-all | bytes 262144 | tf_op jit(solution)/shard_map/all_to_all | solution.py:25
  51.7 0.2 all_to_all.60
  51.9 43.9 %all-gather.2.cloned.1.call-done = bf16[8,512,512]{2,1,0:T(8,128)(2,1)} async-done(((bf16[8,16,512]{2,1,0:T(8,128)(2,1)}), bf16[8,512,512]{2,1,0:T(8,128)(2,1)}) %all-gather.2.cloned.1.call-update) | async-done | bytes 4194320 | tf_op jit(solution)/shard_map/all_gather | solution.py:34
  95.9 2.8 fusion
  98.7 0.8 copy.94
  99.5 1.1 reshape.49
  100.5 18.0 %all_to_all.74 = bf16[8,2,4096]{2,1,0:T(2,128)(2,1)S(1)} all-to-all(bf16[8,2,4096]{2,1,0:T(2,128)(2,1)S(1)} %reshape.49), channel_id=1, replica_groups=mesh['row'=32,'col'=8] {'col'}, dimensions={0} | all-to-all | bytes 262144 | tf_op jit(solution)/shard_map/all_to_all | solution.py:46
  118.6 0.7 reshape.50
  119.3 0.7 copy.95
  120.2 0.3 copy.97
  120.5 0.4 multiply_convert_fusion.4
  120.9 0.3 copy.99
  121.2 0.2 reshape.51
  121.4 13.0 %all_to_all.75 = bf16[8,2,4096]{2,1,0:T(2,128)(2,1)S(1)} all-to-all(bf16[8,2,4096]{2,1,0:T(2,128)(2,1)S(1)} %reshape.51), channel_id=1, replica_groups=mesh['row'=32,'col'=8] {'col'}, dimensions={0} | all-to-all | bytes 262144 | tf_op jit(solution)/shard_map/all_to_all | solution.py:26
  134.8 0.2 all_to_all.65
  135.1 4.5 convolution_bitcast_fusion
  139.6 10.4 %copy.101 = f32[512,8,512]{2,1,0:T(8,128)} copy(f32[512,8,512]{0,2,1:T(8,128)} %convolution_bitcast_fusion) | data formatting | bytes 16777216 | tf_op jit(solution)/shard_map/hij,hik->jhk/transpose | solution.py:39
  150.1 150.5 %reduce-scatter.2.cloned.1.call-done = f32[16,8,512]{2,1,0:T(8,128)} async-done(((f32[512,8,512]{2,1,0:T(8,128)}), f32[16,8,512]{2,1,0:T(8,128)}) %reduce-scatter.2.cloned.1.call-update) | async-done | bytes 262160 | tf_op jit(solution)/shard_map/reduce_scatter | solution.py:38
  300.5 1.0 convert_bitcast_fusion
  301.5 0.8 copy.102
  302.3 1.1 reshape.53
  303.4 16.3 %all_to_all.76 = bf16[8,2,4096]{2,1,0:T(2,128)(2,1)S(1)} all-to-all(bf16[8,2,4096]{2,1,0:T(2,128)(2,1)S(1)} %reshape.53), channel_id=1, replica_groups=mesh['row'=32,'col'=8] {'col'}, dimensions={0} | all-to-all | bytes 262144 | tf_op jit(solution)/shard_map/all_to_all | solution.py:47
  319.7 0.7 reshape.54
  320.4 0.7 copy.103
  321.4 0.3 copy.105
  321.6 0.3 multiply_convert_fusion.1
  322.0 1.5 convolution_bitcast_fusion.1
  323.5 1.0 fusion.21
  324.5 1.3 fusion.9
  325.9 243.5 %all-reduce.2.cloned.1.call-done = f32[128,256]{1,0:T(8,128)} async-done(((f32[128,256]{1,0:T(8,128)}), f32[128,256]{1,0:T(8,128)}) %all-reduce.2.cloned.1.call-update) | async-done | bytes 131088 | tf_op jit(solution)/shard_map/psum | solution.py:61
  569.4 0.9 broadcast_multiply_fusion
  570.4 0.7 copy.110
  571.1 0.7 copy.109
  571.8 0.7 copy.108
  572.5 0.7 copy.107
  (24 shorter events, 1.9 us)
Async XLA Ops:
  7.2 30.9 %copy-start.1 = (bf16[64,16,64]{2,1,0:T(8,128)(2,1)S(1)}, bf16[64,16,64]{2,1,0:T(8,128)(2,1)}, u32[]{:S(2)}) copy-start(bf16[64,16,64]{2,1,0:T(8,128)(2,1)} %param.7) | copy-start | bytes 393220
  7.2 88.7 %all-gather.2.cloned.1.call-start = ((), (), s32[]{:S(2)}) async-start(), calls=%async_computation.6 | async-start | bytes 4325376 | tf_op jit(solution)/shard_map/all_gather | solution.py:34
  38.0 262.5 %reduce-scatter.2.cloned.1.call-start = ((), (), s32[]{:S(2)}) async-start(), calls=%async_computation.7 | async-start | bytes 8650752 | tf_op jit(solution)/shard_map/reduce_scatter | solution.py:38
  150.0 419.4 %all-reduce.2.cloned.1.call-start = ((), (), s32[]{:S(2)}) async-start(), calls=%async_computation.8 | async-start | bytes 262144 | tf_op jit(solution)/shard_map/psum | solution.py:61
  302.3 19.7 %copy-start = (bf16[16,64,128]{2,1,0:T(8,128)(2,1)S(1)}, bf16[16,64,128]{2,1,0:T(8,128)(2,1)}, u32[]{:S(2)}) copy-start(bf16[16,64,128]{2,1,0:T(8,128)(2,1)} %param.6) | copy-start | bytes 786436
Sparse Core Ops, SparseCore 0:
  38.1 57.7 all-gather.1
  150.1 150.3 reduce-scatter.1
  324.7 244.7 all-reduce.1
where the time goes:
time: 581 us; the launch traced here: 580 us
  waiting for transfers between devices  438 us (75%)
  blocking collectives  81.8 us (14%)
  local copies, waits for them, and re-layouts  27.9 us (5%)
  between operations  14 us (2%)
  matrix products  11.3 us (2%)
  other arithmetic  6.66 us (1%)
    psum x1, waiting for transfers between devices, shards(): total_weights = lax.psum(local_weights, ('row', 'col')) / residues  244 us
    reduce_scatter x1, waiting for transfers between devices, shards(): lax.psum_scatter(jnp.einsum('hij,hik->jhk', col_block, left_chan, preferr...  150 us
    all_gather x1, waiting for transfers between devices, shards(): lax.all_gather(right_chan, 'row', axis=1, tiled=True)  43.9 us
    all_to_all x1, blocking collectives, shards(): lax.all_to_all(right, 'col', split_axis=0, concat_axis=2, tiled=True)  21.4 us
    all_to_all x1, blocking collectives, shards(): lax.all_to_all(d_left.astype(jnp.bfloat16), 'col', split_axis=2, concat_a...  18 us
    all_to_all x1, blocking collectives, shards(): lax.all_to_all(d_right.astype(jnp.bfloat16), 'col', split_axis=2, concat_...  16.3 us
    all_to_all x1, blocking collectives, shards(): lax.all_to_all(left, 'col', split_axis=0, concat_axis=2, tiled=True)  13 us
    all_to_all x1, blocking collectives, shards(): lax.all_to_all(cotangent, 'col', split_axis=0, concat_axis=2, tiled=True)  13 us
  transfers between devices with their start and end apart: 3, of which 3 were waited for; matrix products, arithmetic and copies ran while one was open for 0% of the time, Pallas kernels for 0%

commit v1 on v0

--- a/solution.py
+++ b/solution.py
@@ -58,7 +58,7 @@
     local_weights = jnp.einsum(
         "rcd,hrc->dh", normalized_input, grads, preferred_element_type=jnp.float32
     )
-    total_weights = lax.psum(local_weights, ("row", "col")) / residues
+    total_weights = jnp.sum(lax.all_gather(local_weights, ("row", "col")), axis=0) / residues
     normalized_gradient = jnp.einsum(
         "hrc,dh->rcd", grads, stacked, preferred_element_type=jnp.float32
     )

time: 581 us -> 1100 us (1.89)
  waiting for transfers between devices: 438 us -> 940 us
  other arithmetic: 6.66 us -> 17.9 us
    all_gather x0 -> x1, waiting for transfers between devices: none -> 746 us  [shards(): lax.all_gather(local_weights, ('row', 'col'))]
    psum x1 -> x0, waiting for transfers between devices: 244 us -> none  [shards(): total_weights = lax.psum(local_weights, ('row', 'col')) / residues]
    reduce_sum x0 -> x1, other arithmetic: none -> 12.2 us  [shards(): jnp.sum(lax.all_gather(local_weights, ('row', 'col')), axis=0) / residues]
where the time goes in v1:
time: 1100 us; the launch traced here: 1090 us
  waiting for transfers between devices  940 us (85%)
  blocking collectives  81.5 us (7%)
  local copies, waits for them, and re-layouts  28.8 us (3%)
  other arithmetic  17.9 us (2%)
  between operations  14 us (1%)
  matrix products  11.2 us (1%)
    all_gather x1, waiting for transfers between devices, shards(): lax.all_gather(local_weights, ('row', 'col'))  746 us
    reduce_scatter x1, waiting for transfers between devices, shards(): lax.psum_scatter(jnp.einsum('hij,hik->jhk', col_block, left_chan, preferr...  150 us
    all_gather x1, waiting for transfers between devices, shards(): lax.all_gather(right_chan, 'row', axis=1, tiled=True)  43.7 us
  transfers between devices with their start and end apart: 3, of which 3 were waited for; matrix products, arithmetic and copies ran while one was open for 0% of the time, Pallas kernels for 0%

profile of v1, /device:TPU:2, one launch (start us, length us, event | category | flops | bytes accessed | tf_op | source)
XLA Modules:
  0.0 1093.5 jit_solution(17165267375763809610)
XLA Ops:
  7.2 1.2 convert_reduce_fusion
  8.4 1.3 fusion.10
  9.7 0.8 copy.79
  10.6 0.8 copy.80
  11.4 0.8 copy.81
  12.2 0.8 copy.82
  13.1 1.4 fusion.18
  14.5 0.2 multiply_convert_fusion.5
  14.8 0.3 copy.83
  15.0 0.2 reshape.48
  15.3 21.4 %all_to_all.72 = bf16[8,2,4096]{2,1,0:T(2,128)(2,1)S(1)} all-to-all(bf16[8,2,4096]{2,1,0:T(2,128)(2,1)S(1)} %reshape.48), channel_id=1, replica_groups=mesh['row'=32,'col'=8] {'col'}, dimensions={0} | all-to-all | bytes 262144 | tf_op jit(solution)/shard_map/all_to_all | solution.py:27
  36.6 0.2 reshape.49
  37.0 0.9 all_to_all.56
  38.0 1.2 reshape.46
  39.2 13.0 %all_to_all.73 = bf16[8,2,4096]{2,1,0:T(2,128)(2,1)S(1)} all-to-all(bf16[8,2,4096]{2,1,0:T(2,128)(2,1)S(1)} %reshape.46), channel_id=1, replica_groups=mesh['row'=32,'col'=8] {'col'}, dimensions={0} | all-to-all | bytes 262144 | tf_op jit(solution)/shard_map/all_to_all | solution.py:25
  52.2 0.2 reshape.47
  52.8 43.7 %all-gather.4.cloned.1.call-done = bf16[8,512,512]{2,1,0:T(8,128)(2,1)} async-done(((bf16[8,16,512]{2,1,0:T(8,128)(2,1)}), bf16[8,512,512]{2,1,0:T(8,128)(2,1)}) %all-gather.4.cloned.1.call-update) | async-done | bytes 4194320 | tf_op jit(solution)/shard_map/all_gather | solution.py:34
  96.5 2.8 fusion
  99.4 0.8 copy.86
  100.2 1.1 reshape.50
  101.2 17.4 %all_to_all.74 = bf16[8,2,4096]{2,1,0:T(2,128)(2,1)S(1)} all-to-all(bf16[8,2,4096]{2,1,0:T(2,128)(2,1)S(1)} %reshape.50), channel_id=1, replica_groups=mesh['row'=32,'col'=8] {'col'}, dimensions={0} | all-to-all | bytes 262144 | tf_op jit(solution)/shard_map/all_to_all | solution.py:46
  118.6 0.7 reshape.51
  119.3 0.7 copy.87
  120.3 0.3 copy.89
  120.5 0.4 multiply_convert_fusion.4
  120.9 0.3 copy.91
  121.2 0.2 reshape.52
  121.4 13.0 %all_to_all.75 = bf16[8,2,4096]{2,1,0:T(2,128)(2,1)S(1)} all-to-all(bf16[8,2,4096]{2,1,0:T(2,128)(2,1)S(1)} %reshape.52), channel_id=1, replica_groups=mesh['row'=32,'col'=8] {'col'}, dimensions={0} | all-to-all | bytes 262144 | tf_op jit(solution)/shard_map/all_to_all | solution.py:26
  135.1 4.5 convolution_bitcast_fusion
  139.6 10.4 copy.93
  150.1 150.4 %reduce-scatter.2.cloned.1.call-done = f32[16,8,512]{2,1,0:T(8,128)} async-done(((f32[512,8,512]{2,1,0:T(8,128)}), f32[16,8,512]{2,1,0:T(8,128)}) %reduce-scatter.2.cloned.1.call-update) | async-done | bytes 262160 | tf_op jit(solution)/shard_map/reduce_scatter | solution.py:38
  300.5 1.0 convert_bitcast_fusion
  301.5 0.8 copy.94
  302.3 1.1 reshape.54
  303.4 16.7 %all_to_all.76 = bf16[8,2,4096]{2,1,0:T(2,128)(2,1)S(1)} all-to-all(bf16[8,2,4096]{2,1,0:T(2,128)(2,1)S(1)} %reshape.54), channel_id=1, replica_groups=mesh['row'=32,'col'=8] {'col'}, dimensions={0} | all-to-all | bytes 262144 | tf_op jit(solution)/shard_map/all_to_all | solution.py:47
  320.0 0.7 reshape.55
  320.7 0.7 copy.95
  321.7 0.3 copy.97
  322.0 0.3 multiply_convert_fusion.1
  322.3 1.5 convolution_bitcast_fusion.1
  323.8 1.0 fusion.21
  324.8 1.3 fusion.9
  326.1 745.8 %all-gather.6.cloned.1.call-done = f32[32768,256]{1,0:T(8,128)} async-done(((f32[128,256]{1,0:T(8,128)}), f32[32768,256]{1,0:T(8,128)}) %all-gather.6.cloned.1.call-update) | async-done | bytes 33554448 | tf_op jit(solution)/shard_map/all_gather | solution.py:61
  1071.9 12.2 %reduce_sum.49 = f32[128,256]{1,0:T(8,128)S(1)} reduce(f32[256,128,256]{2,1,0:T(8,128)} %bitcast.43, f32[]{:T(128)} %constant.12.clone.1), dimensions={0}, to_apply=%region_5.0 | reduce | flops 8355840 | bytes 33685508 | tf_op jit(solution)/shard_map/reduce_sum | solution.py:61
  1084.2 0.7 copy.102
  1084.9 0.7 copy.101
  1085.6 0.7 copy.100
  1086.3 0.7 copy.99
  (23 shorter events, 1.9 us)
Async XLA Ops:
  7.2 89.4 %all-gather.4.cloned.1.call-start = ((), (), s32[]{:S(2)}) async-start(), calls=%async_computation.6 | async-start | bytes 4325376 | tf_op jit(solution)/shard_map/all_gather | solution.py:34
  37.9 262.6 %reduce-scatter.2.cloned.1.call-start = ((), (), s32[]{:S(2)}) async-start(), calls=%async_computation.7 | async-start | bytes 8650752 | tf_op jit(solution)/shard_map/reduce_scatter | solution.py:38
  150.0 172.3 %copy-start = (bf16[16,64,128]{2,1,0:T(8,128)(2,1)S(1)}, bf16[16,64,128]{2,1,0:T(8,128)(2,1)}, u32[]{:S(2)}) copy-start(bf16[16,64,128]{2,1,0:T(8,128)(2,1)} %param.6) | copy-start | bytes 786436
  150.0 921.8 %all-gather.6.cloned.1.call-start = ((), (), s32[]{:S(2)}) async-start(), calls=%async_computation.8 | async-start | bytes 33685504 | tf_op jit(solution)/shard_map/all_gather | solution.py:61
Sparse Core Ops, SparseCore 0:
  38.1 58.4 all-gather.3
  150.2 150.3 reduce-scatter.1
  323.9 747.8 all-gather.5
